TPU v7x, 32 devices: a whole 2x2x4 slice. The times are simulated.
32 devices in a mesh: gz: 4 (over z), xy: 8 (over y, x, core).
Axes of the slice: x: 2, y: 2, z: 4, core: 2. Of those that a mesh axis runs over, the one named last changes fastest.
Arguments:
- features: bfloat16 [48, 16, 160, 256], P(None, 'gz', 'xy'), may hold values from -6 to 6
- first_weight: bfloat16 [3, 3, 3, 48, 48], replicated, may hold values from -0.15625 to 0.15625
- first_bias: float32 [48], replicated, may hold values from -0.5 to 0.5
- second_weight: bfloat16 [3, 3, 3, 64, 48], replicated, may hold values from -0.15625 to 0.15625
- second_bias: float32 [64], replicated, may hold values from -0.5 to 0.5
- labels: int32 [16, 160, 256], P('gz', 'xy'), may hold values from 0 to 4095, as said below
- blocks: int32 [4, 8, 256, 128], P('gz', 'xy'), may hold values from -1 to 20479, as said below
- owner_map: int32 [4096], replicated, may hold values from 0 to 4095, as said below
Outputs:
- mean_embedding: float32 [4096, 64], P(('gz', 'xy'))
- covariance: float32 [4096, 4096], P(('gz', 'xy'))
Inputs may be any that keep to these rules, and one draw needn't show every extreme that they name: `labels`: all voxels listed in one block carry the same label. A tile's 256 blocks together list every voxel of the tile exactly once. A block lists a quarter of 128 to 128 voxels whose indices follow one another in ascending order, then -1 to its end. In each tile at most 24 blocks have rows owner_map[label] within one device's 128 output rows, and in every draw the rows of some devices receive exactly 24 blocks from every tile. `owner_map`: A permutation of the output rows.
All inputs are finite; a program needn't handle non-finite values.
Results may differ from a plain program's by a relative error of at most 0.0042.
Values may be sent and summed in bfloat16 or wider, within the bound.
No kernel may reach another device: no remote copies, remote signals or barrier semaphores. Data moves between devices by JAX's collectives and lax.ppermute only.
A program may use at most 128 MiB of HBM per device.

v0:
```python
import jax
import jax.numpy as jnp
import numpy as np
from jax import lax
from jax.sharding import PartitionSpec as P

SV_DEV = 128


CONV_LAYOUT = ("NCDHW", "DHWOI", "NCDHW")


def extended(array, sides, width):
    for axis, dim in sides:
        devices, length = (lax.axis_size(axis), array.shape[dim])
        up = [(i, (i + 1) % devices) for i in range(devices - 1)]
        down = [(j, i) for i, j in up]
        last = lax.slice_in_dim(array, length - width, length, axis=dim)
        leading = lax.slice_in_dim(array, 0, width, axis=dim)
        before = lax.ppermute(last, axis, up)
        after = lax.ppermute(leading, axis, down)
        array = jnp.concatenate([before, array, after], axis=dim)
    return array


def convolve(padded, weight, bias):
    summed = lax.conv_general_dilated(
        padded[None],
        weight,
        (1, 1, 1),
        ((0, 0), (0, 0), (1, 1)),
        dimension_numbers=CONV_LAYOUT,
        preferred_element_type=jnp.float32,
    )[0]
    return summed + bias[:, None, None, None]


def triangle_tables(width):
    upper_rows, upper_cols = np.triu_indices(width)
    position = np.zeros((width, width), np.int32)
    position[upper_rows, upper_cols] = np.arange(upper_rows.shape[0], dtype=np.int32)
    position[upper_cols, upper_rows] = np.arange(upper_rows.shape[0], dtype=np.int32)
    return ((upper_rows * width + upper_cols).astype(np.int32), position.reshape(-1))


def pick_slots(values, slot_block, filler):
    extra = jnp.full((1,) + values.shape[1:], filler, values.dtype)
    return jnp.concatenate([values, extra], axis=0)[slot_block]


def local(
    features, first_weight, first_bias, second_weight, second_bias, labels, blocks, owner_map
):
    padded = extended(features, (("gz", 1), ("xy", 2)), 1)
    hidden = jax.nn.relu(convolve(padded, first_weight, first_bias)).astype(jnp.bfloat16)
    hidden_pad = extended(hidden, (("gz", 1), ("xy", 2)), 1)
    embedding = convolve(hidden_pad, second_weight, second_bias).astype(jnp.bfloat16)
    channels = embedding.shape[0]
    flat_embed = embedding.reshape(channels, -1)
    block_count = blocks.shape[2]
    block_width = blocks.shape[3]
    voxel_lists = blocks.reshape(block_count, block_width)
    in_block = voxel_lists >= 0
    picked = jnp.take(flat_embed, jnp.where(in_block, voxel_lists, 0).reshape(-1), axis=1).reshape(
        channels, block_count, block_width
    )
    picked = jnp.where(in_block[None], picked, jnp.zeros((), jnp.bfloat16))
    block_sizes = jnp.sum(in_block.astype(jnp.float32), axis=1)
    block_sums = jnp.einsum("cnk->nc", picked, preferred_element_type=jnp.float32)
    block_second = jnp.einsum(
        "cnk,dnk->ncd", picked, picked, preferred_element_type=jnp.float32
    ).reshape(block_count, channels * channels)
    owner_rows = owner_map[labels.reshape(-1)[voxel_lists[:, 0]]]
    depth_count = lax.axis_size("gz")
    plane_count = lax.axis_size("xy")
    devices = depth_count * plane_count
    capacity = max(2, 3 * block_count // devices)
    target_dev = owner_rows // SV_DEV
    local_rows = owner_rows % SV_DEV
    target_hits = (target_dev[:, None] == jnp.arange(devices, dtype=jnp.int32)[None, :]).astype(
        jnp.int32
    )
    slot_rank = jnp.sum((jnp.cumsum(target_hits, axis=0) - target_hits) * target_hits, axis=1)
    slot_block = (
        jnp.full((devices * capacity,), block_count, jnp.int32)
        .at[target_dev * capacity + slot_rank]
        .set(jnp.arange(block_count, dtype=jnp.int32))
    )
    flat_upper, expand_back = triangle_tables(channels)
    block_second = jnp.take(block_second, jnp.asarray(flat_upper), axis=1)
    send_sizes = pick_slots(block_sizes, slot_block, 0.0)
    send_rows = pick_slots(local_rows.astype(jnp.float32), slot_block, float(SV_DEV))
    send_sums = pick_slots(block_sums, slot_block, 0.0)
    send_second = pick_slots(block_second, slot_block, 0.0)
    moment_width = send_second.shape[1]
    arrived = (
        lax.all_to_all(
            send_sizes.reshape(devices, capacity),
            ("gz", "xy"),
            split_axis=0,
            concat_axis=0,
            tiled=True,
        ),
        lax.all_to_all(
            send_rows.reshape(devices, capacity),
            ("gz", "xy"),
            split_axis=0,
            concat_axis=0,
            tiled=True,
        ),
        lax.all_to_all(
            send_sums.reshape(devices, capacity, channels),
            ("gz", "xy"),
            split_axis=0,
            concat_axis=0,
            tiled=True,
        ),
        lax.all_to_all(
            send_second.reshape(devices, capacity, moment_width),
            ("gz", "xy"),
            split_axis=0,
            concat_axis=0,
            tiled=True,
        ),
    )
    got_sizes = arrived[0].reshape(devices * capacity)
    got_rows = arrived[1].reshape(devices * capacity).astype(jnp.int32)
    got_sums = arrived[2].reshape(devices * capacity, channels)
    got_second = arrived[3].reshape(devices * capacity, moment_width)
    row_hits = (got_rows[:, None] == jnp.arange(SV_DEV, dtype=jnp.int32)[None, :]).astype(
        jnp.float32
    )
    total_sizes = jnp.einsum("rs,r->s", row_hits, got_sizes, precision=lax.Precision.HIGHEST)
    total_sums = jnp.einsum("rs,rc->sc", row_hits, got_sums, precision=lax.Precision.HIGHEST)
    total_second = jnp.einsum("rs,rc->sc", row_hits, got_second, precision=lax.Precision.HIGHEST)
    total_second = jnp.take(total_second, jnp.asarray(expand_back), axis=1)
    denominator = jnp.maximum(total_sizes, 1.0)
    mean_embedding = total_sums / denominator[:, None]
    covariance = total_second / denominator[:, None] - (
        mean_embedding[:, :, None] * mean_embedding[:, None, :]
    ).reshape(SV_DEV, channels * channels)
    return (mean_embedding, covariance)


def solution(mesh):
    return jax.shard_map(
        local,
        mesh=mesh,
        in_specs=(
            P(None, "gz", "xy", None),
            P(),
            P(),
            P(),
            P(),
            P("gz", "xy", None),
            P("gz", "xy", None, None),
            P(),
        ),
        out_specs=(P(("gz", "xy"), None), P(("gz", "xy"), None)),
        check_vma=False,
    )
```

profile of v0, /device:TPU:0, one launch (start us, length us, event | category | flops | bytes accessed | tf_op | source)
XLA Modules:
  0.0 655.6 jit_solution(13296760123429344043)
XLA Ops:
  0.7 3.9 fusion.50
  4.7 5.8 collective-permute-start
  12.9 1.7 gather_fusion
  14.7 1.7 gather_fusion.1
  18.9 5.0 gather_fusion.2
  24.6 7.0 %all-to-all-start = ((f32[32,1,24]{2,1,0:T(1,128)}), f32[32,1,24]{2,1,0:T(1,128)}, u32[]{:S(2)}, u32[]{:S(2)}) async-start(f32[32,1,24]{2,1,0:T(1,128)} %bitcast.9), calls=%async_computation | async-start | bytes 32768 | tf_op jit(solution)/shard_map/all_to_all | solution.py:104
  31.6 1.8 copy.41
  33.4 1.8 copy.42
  35.6 2.1 collective-permute-start.2
  40.0 2.1 collective-permute-done.3
  42.1 3.4 maximum_bitcast_fusion
  45.5 5.6 pad.2
  51.1 19.5 %reshape.337 = bf16[48,6,22,1,8,33]{5,4,1,2,0,3:T(8,128)(2,1)} reshape(bf16[48,6,22,1,264]{4,1,2,0,3:T(8,128)(2,1)} %pad.2) | data formatting | bytes 6690816 | tf_op jit(solution)/shard_map/conv_general_dilated | solution.py:27
  70.6 18.3 %copy.45 = bf16[48,6,22,1,8,33]{0,4,5,2,1,3:T(8,128)(2,1)} copy(bf16[48,6,22,1,8,33]{5,4,1,2,0,3:T(8,128)(2,1)} %reshape.337) | data formatting | bytes 6690816 | tf_op jit(solution)/shard_map/conv_general_dilated | solution.py:27
  90.2 31.1 %broadcast_select_fusion.1 = f32[4,20,8,33,48]{4,2,3,1,0:T(8,128)} fusion(pred[8,33]{0,1:T(8,128)(4,1)S(1)} %copy-done.13, bf16[3,3,3,48,48]{4,3,2,1,0:T(8,128)(2,1)S(1)} %copy-done.12, bf16[48,6,22,1,7,2]{0,4,5,2,1,3:T(8,128)(2,1)S(1)} %slice.68, bf16[48,6,22,1,8,33]{0,4,5,2,1,3:T(8,128)(2,1)} %copy.45), kind=kOutput, calls=%fused_computation.30 | convolution fusion | flops 2639324160 | bytes 7702536 | tf_op jit(solution)/shard_map/conv_general_dilated | solution.py:27
  121.2 14.2 %copy.46 = f32[4,20,8,33,48]{3,2,4,1,0:T(8,128)} copy(f32[4,20,8,33,48]{4,2,3,1,0:T(8,128)} %broadcast_select_fusion.1) | data formatting | bytes 8110080 | tf_op jit(solution)/shard_map/conv_general_dilated | solution.py:27
  135.4 13.1 %reshape.232 = f32[4,20,1,264,48]{3,4,1,0,2:T(8,128)} reshape(f32[4,20,8,33,48]{3,2,4,1,0:T(8,128)} %copy.46) | data formatting | bytes 8110080 | tf_op jit(solution)/shard_map/conv_general_dilated | solution.py:27
  148.5 2.7 fusion.21
  151.3 3.4 collective-permute-start.4
  156.8 6.3 collective-permute-done.4
  163.1 4.7 collective-permute-done.5
  168.5 5.3 collective-permute-start.6
  176.9 16.8 %gather_fusion.5 = f32[768]{0:T(1024)S(1)} fusion(f32[257]{0:T(512)S(1)} %pad_maximum_fusion.7, s32[1024]{0:T(1024)S(1)} %pad_clamp_fusion.1), kind=kCustom, calls=%fused_computation.5 | custom fusion | bytes 9216 | tf_op jit(solution)/shard_map/gather | solution.py:48
  196.7 4.4 pad.4
  201.2 17.9 %reshape.235 = bf16[48,6,22,1,8,33]{5,4,0,2,1,3:T(8,128)(2,1)} reshape(bf16[48,6,22,1,264]{4,0,2,1,3:T(8,128)(2,1)} %pad.4) | data formatting | bytes 6690816 | tf_op jit(solution)/shard_map/conv_general_dilated | solution.py:27
  219.0 18.1 %copy.48 = bf16[48,6,22,1,8,33]{0,4,5,2,1,3:T(8,128)(2,1)} copy(bf16[48,6,22,1,8,33]{5,4,0,2,1,3:T(8,128)(2,1)} %reshape.235) | data formatting | bytes 6690816 | tf_op jit(solution)/shard_map/conv_general_dilated | solution.py:27
  238.3 29.6 %broadcast_select_fusion = f32[4,20,8,33,64]{4,2,3,1,0:T(8,128)S(1)} fusion(pred[8,33]{0,1:T(8,128)(4,1)S(1)} %copy-done.14, bf16[3,3,3,64,48]{3,4,2,1,0:T(8,128)(2,1)S(1)} %copy-done, bf16[48,6,22,1,7,2]{0,4,5,2,1,3:T(8,128)(2,1)S(1)} %slice.72, bf16[48,6,22,1,8,33]{0,4,5,2,1,3:T(8,128)(2,1)} %copy.48), kind=kOutput, calls=%fused_computation.29 | convolution fusion | flops 3515550720 | bytes 9095688 | tf_op jit(solution)/shard_map/conv_general_dilated | solution.py:27
  268.0 8.5 %copy.49 = f32[4,20,8,33,64]{4,0,3,2,1:T(4,128)} copy(f32[4,20,8,33,64]{4,2,3,1,0:T(8,128)S(1)} %broadcast_select_fusion) | data formatting | bytes 10813440 | tf_op jit(solution)/shard_map/conv_general_dilated | solution.py:27
  276.4 8.8 %slice_bitcast_fusion = f32[1,64,4,20,256]{1,2,4,3,0:T(4,128)} fusion(f32[4,20,1,264,64]{4,0,3,1,2:T(4,128)} %bitcast.106), kind=kLoop, calls=%fused_computation.13 | loop fusion | bytes 10485760 | tf_op jit(solution)/shard_map/conv_general_dilated | solution.py:27
  285.3 5.4 copy.50
  290.7 3.0 fusion.2
  293.7 113.5 %gather_fusion.3 = bf16[32768,64]{1,0:T(8,128)(2,1)} fusion(bf16[64,20480]{0,1:T(8,128)(2,1)} %fusion.2, s32[32768]{0:T(1024)S(1)} %broadcast_clamp_fusion), kind=kCustom, calls=%fused_computation.3 | custom fusion | bytes 8519680 | tf_op jit(solution)/shard_map/jit(_take)/gather | solution.py:64
  407.2 8.6 %copy.51 = bf16[64,256,128]{2,0,1:T(8,128)(2,1)} copy(bf16[64,256,128]{0,2,1:T(8,128)(2,1)} %bitcast.108) | data formatting | bytes 8388608 | tf_op jit(solution)/shard_map/jit(_take)/gather | solution.py:64
  415.8 9.4 %all-to-all-start.2 = ((f32[32,1,24]{2,1,0:T(1,128)}), f32[32,1,24]{2,1,0:T(1,128)S(1)}, u32[]{:S(2)}, u32[]{:S(2)}) async-start(f32[32,1,24]{2,1,0:T(1,128)} %bitcast.26), calls=%async_computation.2 | async-start | bytes 32768 | tf_op jit(solution)/shard_map/all_to_all | solution.py:97
  425.2 4.4 convert_reduce_fusion
  432.3 5.7 all-to-all-start.1
  438.0 9.1 %fusion.26 = f32[256,64,64]{2,1,0:T(8,128)} fusion(bf16[64,256,128]{2,0,1:T(8,128)(2,1)} %copy.51, pred[256,128]{1,0:T(8,128)(4,1)S(1)} %copy.38, pred[256,128]{1,0:T(8,128)(4,1)S(1)} %copy.37), kind=kOutput, calls=%fused_computation.40 | convolution fusion | flops 272629760 | bytes 8454144 | tf_op jit(solution)/shard_map/cnk,dnk->ncd/dot_general | solution.py:70
  447.0 7.8 %copy.53 = f32[256,64,64]{0,2,1:T(8,128)} copy(f32[256,64,64]{2,1,0:T(8,128)} %fusion.26) | data formatting | bytes 8388608 | tf_op jit(solution)/shard_map/cnk,dnk->ncd/dot_general | solution.py:70
  454.8 7.5 %gather_fusion.6 = f32[2080,256]{1,0:T(8,128)S(1)} fusion(f32[256,4096]{0,1:T(8,128)} %bitcast.105, s32[3072]{0:T(1024)S(1)} %pad_clamp_fusion), kind=kCustom, calls=%fused_computation.6 | custom fusion | bytes 4268160 | tf_op jit(solution)/shard_map/jit(_take)/gather | solution.py:90
  462.3 1.9 copy.60
  464.3 1.8 concatenate.31.clone
  466.0 5.5 gather_fusion.7
  471.5 6.2 all-to-all-start.3
  482.9 143.3 %all-to-all-done.3 = f32[32,24,2080]{2,1,0:T(8,128)} async-done(((f32[32,24,2080]{2,1,0:T(8,128)}), f32[32,24,2080]{2,1,0:T(8,128)}, u32[]{:S(2)}, u32[]{:S(2)}) %all-to-all-start.3) | async-done | bytes 6389792 | tf_op jit(solution)/shard_map/all_to_all | solution.py:118
  626.2 8.5 %fusion.30 = f32[128,2080]{0,1:T(8,128)S(1)} fusion(f32[768,2080]{1,0:T(8,128)} %bitcast.31, s32[768]{0:T(1024)S(1)} %convert_element_type.38), kind=kOutput, calls=%fused_computation.51 | convolution fusion | flops 2453766144 | bytes 7457792 | tf_op jit(solution)/shard_map/rs,rc->sc/dot_general | solution.py:135
  634.7 14.2 %gather_fusion.8 = f32[4096,128]{1,0:T(8,128)} fusion(f32[128,2080]{0,1:T(8,128)S(1)} %fusion.30, s32[4096]{0:T(1024)S(1)} %broadcast_clamp_fusion.1), kind=kCustom, calls=%fused_computation.8 | custom fusion | bytes 4210688 | tf_op jit(solution)/shard_map/jit(_take)/gather | solution.py:136
  648.9 3.4 bitcast_subtract_fusion
  652.3 2.9 copy.55
  (96 shorter events, 27.4 us)
Async XLA Ops:
  0.6 237.7 %copy-start = (bf16[3,3,3,64,48]{3,4,2,1,0:T(8,128)(2,1)S(1)}, bf16[3,3,3,64,48]{3,4,2,1,0:T(8,128)(2,1)}, u32[]{:S(2)}) copy-start(bf16[3,3,3,64,48]{3,4,2,1,0:T(8,128)(2,1)} %param.13) | copy-start | bytes 497668
  0.6 12.1 %copy-start.4 = (s32[1,1,256,128]{3,2,1,0:T(8,128)S(1)}, s32[1,1,256,128]{3,2,1,0:T(8,128)}, u32[]{:S(2)}) copy-start(s32[1,1,256,128]{3,2,1,0:T(8,128)} %param.16) | copy-start | bytes 393220
  0.7 12.2 %copy-start.8 = (s32[4,20,256]{2,0,1:T(4,128)S(1)}, s32[4,20,256]{2,0,1:T(4,128)}, u32[]{:S(2)}) copy-start(s32[4,20,256]{2,0,1:T(4,128)} %param.15) | copy-start | bytes 245764
  0.7 14.0 %copy-start.2 = (s32[4096]{0:T(1024)S(1)}, s32[4096]{0:T(1024)}, u32[]{:S(2)}) copy-start(s32[4096]{0:T(1024)} %param.17) | copy-start | bytes 49156
  4.7 26.9 %collective-permute-start = (bf16[48,1,20,256]{3,0,2,1:T(8,128)(2,1)S(1)}, bf16[48,1,20,256]{3,0,2,1:T(8,128)(2,1)}, u32[]{:S(2)}, u32[]{:S(2)}) collective-permute-start(bf16[48,1,20,256]{3,0,2,1:T(8,128)(2,1)S(1)} %copy.58), channel_id=1, source_target_pairs={{0,8},{8,16},{16,24},{1,9},{9,17},{17,25},{2,10},{10,18},{18,26},{... | collective-permute-start | bytes 1474568 | tf_op jit(solution)/shard_map/ppermute | solution.py:20
  11.4 22.0 %collective-permute-start.1 = (bf16[48,1,20,256]{3,0,2,1:T(8,128)(2,1)}, bf16[48,1,20,256]{3,0,2,1:T(8,128)(2,1)}, u32[]{:S(2)}, u32[]{:S(2)}) collective-permute-start(bf16[48,1,20,256]{3,0,2,1:T(8,128)(2,1)} %copy.59), channel_id=1, source_target_pairs={{8,0},{16,8},{24,16},{9,1},{17,9},{25,17},{10,2},{18,10},{26,18},{... | collective-permute-start | bytes 1474568 | tf_op jit(solution)/shard_map/ppermute | solution.py:21
  12.9 22.3 %copy-start.3 = (bf16[48,4,20,256]{3,1,2,0:T(4,128)(2,1)S(1)}, bf16[48,4,20,256]{3,1,2,0:T(4,128)(2,1)}, u32[]{:S(2)}) copy-start(bf16[48,4,20,256]{3,1,2,0:T(4,128)(2,1)} %param.10) | copy-start | bytes 5898244
  24.6 391.2 %all-to-all-start = ((f32[32,1,24]{2,1,0:T(1,128)}), f32[32,1,24]{2,1,0:T(1,128)}, u32[]{:S(2)}, u32[]{:S(2)}) async-start(f32[32,1,24]{2,1,0:T(1,128)} %bitcast.9), calls=%async_computation | async-start | bytes 32768 | tf_op jit(solution)/shard_map/all_to_all | solution.py:104
  35.6 4.5 collective-permute-start.2
  37.7 4.5 collective-permute-start.3
  70.6 19.6 %copy-start.12 = (bf16[3,3,3,48,48]{4,3,2,1,0:T(8,128)(2,1)S(1)}, bf16[3,3,3,48,48]{4,3,2,1,0:T(8,128)(2,1)}, u32[]{:S(2)}) copy-start(bf16[3,3,3,48,48]{4,3,2,1,0:T(8,128)(2,1)} %param.11) | copy-start | bytes 373252
  70.6 19.6 %copy-start.13 = (pred[8,33]{0,1:T(8,128)(4,1)S(1)}, pred[8,33]{0,1:T(8,128)(4,1)}, u32[]{:S(2)}) copy-start(pred[8,33]{0,1:T(8,128)(4,1)} %constant.125) | copy-start | bytes 796
  135.4 13.1 %copy-start.11 = (f32[48]{0:T(128)S(1)}, f32[48]{0:T(128)}, u32[]{:S(2)}) copy-start(f32[48]{0:T(128)} %param.12) | copy-start | bytes 580
  148.5 7.5 %copy-start.5 = (s32[32768,1]{0,1:T(1,128)S(1)}, s32[32768,1]{0,1:T(1,128)}, u32[]{:S(2)}) copy-start(s32[32768,1]{0,1:T(1,128)} %compare_select_fusion) | copy-start | bytes 393220
  151.3 11.8 %collective-permute-start.4 = (bf16[48,1,20,256]{3,0,2,1:T(8,128)(2,1)S(1)}, bf16[48,1,20,256]{3,0,2,1:T(8,128)(2,1)S(1)}, u32[]{:S(2)}, u32[]{:S(2)}) collective-permute-start(bf16[48,1,20,256]{3,0,2,1:T(8,128)(2,1)S(1)} %get-tuple-element.14), channel_id=1, source_target_pairs={{0,8},{8,16},{16,24},{1,9},{9,17},{17,25},{2,10},{10,18},{18,26},{... | collective-permute-start | bytes 1474568 | tf_op jit(solution)/shard_map/ppermute | solution.py:20
  154.7 13.1 %collective-permute-start.5 = (bf16[48,1,20,256]{3,0,2,1:T(8,128)(2,1)S(1)}, bf16[48,1,20,256]{3,0,2,1:T(8,128)(2,1)S(1)}, u32[]{:S(2)}, u32[]{:S(2)}) collective-permute-start(bf16[48,1,20,256]{3,0,2,1:T(8,128)(2,1)S(1)} %get-tuple-element.15), channel_id=1, source_target_pairs={{8,0},{16,8},{24,16},{9,1},{17,9},{25,17},{10,2},{18,10},{26,18},{... | collective-permute-start | bytes 1474568 | tf_op jit(solution)/shard_map/ppermute | solution.py:21
  156.1 19.0 %copy-start.6 = (pred[256,128]{0,1:T(8,128)(4,1)}, pred[256,128]{0,1:T(8,128)(4,1)S(1)}, u32[]{:S(2)}) copy-start(pred[256,128]{0,1:T(8,128)(4,1)S(1)} %get-tuple-element.9) | copy-start | bytes 98308
  168.5 26.6 %collective-permute-start.6 = (bf16[48,6,1,256]{3,0,2,1:T(8,128)(2,1)}, bf16[48,6,1,256]{3,0,2,1:T(8,128)(2,1)}, u32[]{:S(2)}, u32[]{:S(2)}) collective-permute-start(bf16[48,6,1,256]{3,0,2,1:T(8,128)(2,1)} %get-tuple-element.12), channel_id=1, source_target_pairs={{0,1},{1,2},{2,3},{3,4},{4,5},{5,6},{6,7},{8,9},{9,10},{10,11},{11... | collective-permute-start | bytes 442376 | tf_op jit(solution)/shard_map/ppermute | solution.py:20
  173.8 21.3 %collective-permute-start.7 = (bf16[48,6,1,256]{3,0,2,1:T(8,128)(2,1)}, bf16[48,6,1,256]{3,0,2,1:T(8,128)(2,1)}, u32[]{:S(2)}, u32[]{:S(2)}) collective-permute-start(bf16[48,6,1,256]{3,0,2,1:T(8,128)(2,1)} %get-tuple-element.13), channel_id=1, source_target_pairs={{1,0},{2,1},{3,2},{4,3},{5,4},{6,5},{7,6},{9,8},{10,9},{11,10},{12... | collective-permute-start | bytes 442376 | tf_op jit(solution)/shard_map/ppermute | solution.py:21
  219.0 19.3 %copy-start.14 = (pred[8,33]{0,1:T(8,128)(4,1)S(1)}, pred[8,33]{0,1:T(8,128)(4,1)}, u32[]{:S(2)}) copy-start(pred[8,33]{0,1:T(8,128)(4,1)} %constant.125) | copy-start | bytes 796
  285.3 5.4 copy-start.10
  415.8 16.5 %all-to-all-start.2 = ((f32[32,1,24]{2,1,0:T(1,128)}), f32[32,1,24]{2,1,0:T(1,128)S(1)}, u32[]{:S(2)}, u32[]{:S(2)}) async-start(f32[32,1,24]{2,1,0:T(1,128)} %bitcast.26), calls=%async_computation.2 | async-start | bytes 32768 | tf_op jit(solution)/shard_map/all_to_all | solution.py:97
  432.3 39.2 %all-to-all-start.1 = ((f32[32,1,1536]{2,1,0:T(1,128)}), f32[32,1,1536]{2,1,0:T(1,128)S(1)}, u32[]{:S(2)}, u32[]{:S(2)}) async-start(f32[32,1,1536]{2,1,0:T(1,128)} %reshape.357), calls=%async_computation.1 | async-start | bytes 393216 | tf_op jit(solution)/shard_map/all_to_all | solution.py:111
  471.5 6.2 copy-start.9
  471.5 154.7 %all-to-all-start.3 = ((f32[32,24,2080]{2,1,0:T(8,128)}), f32[32,24,2080]{2,1,0:T(8,128)}, u32[]{:S(2)}, u32[]{:S(2)}) async-start(f32[32,24,2080]{2,1,0:T(8,128)} %bitcast.107), calls=%async_computation.3 | async-start | bytes 13369344 | tf_op jit(solution)/shard_map/all_to_all | solution.py:118
  482.6 152.1 %copy-start.7 = (f32[128,64]{0,1:T(8,128)}, f32[128,64]{0,1:T(8,128)S(1)}, u32[]{:S(2)}) copy-start(f32[128,64]{0,1:T(8,128)S(1)} %convolution_divide_fusion) | copy-start | bytes 98308
  634.7 20.5 %copy-start.1 = (bf16[3,3,3,64,48]{3,4,2,1,0:T(8,128)(2,1)S(1)}, bf16[3,3,3,64,48]{3,4,2,1,0:T(8,128)(2,1)}, u32[]{:S(2)}) copy-start(bf16[3,3,3,64,48]{3,4,2,1,0:T(8,128)(2,1)} %param.13) | copy-start | bytes 497668
where the time goes:
time: 664 us; the launch traced here: 656 us
  local copies, waits for them, and re-layouts  342 us (52%)
  waiting for transfers between devices  157 us (24%)
  matrix products  79.2 us (12%)
  starting transfers between devices  50.2 us (8%)
  other arithmetic  25.5 us (4%)
    all_to_all x1, waiting for transfers between devices, local(): lax.all_to_all(send_second.reshape(devices, capacity, moment_width), ('gz...  143 us
    conv_general_dilated x11, local copies, waits for them, and re-layouts, convolve(): lax.conv_general_dilated(padded[None], weight, (1, 1, 1), ((0, 0), (0, 0)...  126 us
    gather x2, local copies, waits for them, and re-layouts, local(): jnp.take(flat_embed, jnp.where(in_block, voxel_lists, 0).reshape(-1), axi...  122 us
    conv_general_dilated x2, matrix products, convolve(): lax.conv_general_dilated(padded[None], weight, (1, 1, 1), ((0, 0), (0, 0)...  60.7 us
    gather x4, local copies, waits for them, and re-layouts, pick_slots(): return jnp.concatenate([values, extra], axis=0)[slot_block]  28.9 us
    ppermute x4, starting transfers between devices, extended(): before = lax.ppermute(last, axis, up)  16.5 us
    gather x1, local copies, waits for them, and re-layouts, local(): total_second = jnp.take(total_second, jnp.asarray(expand_back), axis=1)  14.2 us
  transfers between devices with their start and end apart: 12, of which 5 were waited for; matrix products, arithmetic and copies ran while one was open for 63% of the time, Pallas kernels for 0%

commit v1 on v0

v1 whole, which is shorter than its diff:
```python
import functools

import jax
import jax.numpy as jnp
from jax import lax
from jax.experimental import pallas as pl
from jax.experimental.pallas import tpu as pltpu
from jax.sharding import PartitionSpec as P

BF16 = jnp.bfloat16
F32 = jnp.float32
EMPTY = -200.0
ROW_LANE = 65


def dot_nn(a, b):
    return lax.dot_general(a, b, (((1,), (0,)), ((), ())), preferred_element_type=F32)


def dot_nt(a, b):
    return lax.dot_general(a, b, (((1,), (1,)), ((), ())), preferred_element_type=F32)


def regroup_kernel(x_ref, o_ref, tmp_ref):
    channels, _, rows, length = x_ref.shape
    for c in range(channels):
        value = x_ref[c, 0].astype(F32)
        for half in range(length // 128):
            part = value[:, half * 128:(half + 1) * 128]
            tmp_ref[half, pl.ds(c, rows, stride=channels), :] = part
    for half in range(length // 128):
        o_ref[0, :, half * 128:(half + 1) * 128] = tmp_ref[half].astype(BF16)


def regroup(features):
    channels, depth, rows, length = features.shape
    return pl.pallas_call(
        regroup_kernel,
        grid=(depth,),
        out_shape=jax.ShapeDtypeStruct((depth, rows * channels, length), BF16),
        in_specs=[pl.BlockSpec((channels, 1, rows, length), lambda z: (0, z, 0, 0))],
        out_specs=pl.BlockSpec((1, rows * channels, length), lambda z: (z, 0, 0)),
        scratch_shapes=[pltpu.VMEM((length // 128, rows * channels, 128), F32)],
        compiler_params=pltpu.CompilerParams(vmem_limit_bytes=48 << 20),
    )(features)


def shift_sum(raw, out):
    left, mid, right = raw[:out], raw[out:2 * out], raw[2 * out:]
    length = raw.shape[1]
    lane = lax.broadcasted_iota(jnp.int32, (out, length), 1)
    left = jnp.where(lane == 0, 0.0, pltpu.roll(left, 1, 1))
    right = jnp.where(lane == length - 1, 0.0, pltpu.roll(right, length - 1, 1))
    return mid + left + right


def tile_kernel(
    dims, meta_ref, inv_ref, place_ref, centre, below, above, before, after, c00, c01, c10, c11,
    w1_ref, w2_ref, b1_ref, b2_ref, out_ref,
    feat, hid, emb, moments, extras, sems,
):
    depth, rows, cin, mid, ech, length, devices, slots, blocks = dims
    wide, tall = rows + 4, depth + 4
    lo, hi = 2 * cin, (rows + 2) * cin
    end = wide * cin
    copies = [
        (centre, feat.at[2:depth + 2, lo:hi]),
        (below, feat.at[0:2, lo:hi]),
        (above, feat.at[depth + 2:tall, lo:hi]),
        (before, feat.at[2:depth + 2, 0:lo]),
        (after, feat.at[2:depth + 2, hi:end]),
        (c00, feat.at[0:2, 0:lo]),
        (c01, feat.at[0:2, hi:end]),
        (c10, feat.at[depth + 2:tall, 0:lo]),
        (c11, feat.at[depth + 2:tall, hi:end]),
    ]
    copies = [pltpu.make_async_copy(s, d, sems.at[k]) for k, (s, d) in enumerate(copies)]
    for copy in copies:
        copy.start()

    aug = emb.shape[1]
    tail = jnp.where(lax.broadcasted_iota(jnp.int32, (aug - ech, 128), 0) == 0, 1.0, 0.0).astype(BF16)

    @pl.loop(0, emb.shape[0])
    def _(w):
        emb[w, ech:aug, :] = tail

    emb[emb.shape[0] - 1, 0:ech, :] = jnp.zeros((ech, 128), BF16)

    @pl.loop(0, moments.shape[0] // 64)
    def _(k):
        moments[pl.ds(k * 64, 64), :] = jnp.zeros((64, 128), F32)

    empty = jnp.where(lax.broadcasted_iota(jnp.int32, (8, 128), 1) == ROW_LANE, EMPTY, 0.0)

    @pl.loop(0, extras.shape[0] // 8)
    def _(k):
        extras[pl.ds(k * 8, 8), :] = empty

    for copy in copies:
        copy.wait()

    g, j = place_ref[0], place_ref[1]
    last_g, last_j = place_ref[2], place_ref[3]
    hrows = rows + 2
    for hz in range(depth + 2):
        dead_z = False
        if hz == 0:
            dead_z = g == 0
        if hz == depth + 1:
            dead_z = g == last_g

        @pl.loop(0, hrows, unroll=2)
        def _(hy):
            at = pl.multiple_of(hy * cin, 16)
            slab = jnp.concatenate([feat[hz + k, pl.ds(at, 3 * cin), :] for k in range(3)], axis=0)
            value = shift_sum(dot_nn(w1_ref[...], slab), mid) + b1_ref[...]
            value = jnp.maximum(value, 0.0)
            dead = ((hy == 0) & (j == 0)) | ((hy == hrows - 1) & (j == last_j)) | dead_z
            value = value * jnp.where(dead, 0.0, 1.0)
            hid[hz, pl.ds(pl.multiple_of(hy * mid, 16), mid), :] = value.astype(BF16)

    for z in range(depth):

        @pl.loop(0, rows, unroll=2)
        def _(y):
            at = pl.multiple_of(y * mid, 16)
            slab = jnp.concatenate([hid[z + k, pl.ds(at, 3 * mid), :] for k in range(3)], axis=0)
            value = (shift_sum(dot_nn(w2_ref[...], slab), ech) + b2_ref[...]).astype(BF16)
            parts = length // 128
            for p in range(parts):
                emb[(z * rows + y) * parts + p, 0:ech, :] = value[:, p * 128:(p + 1) * 128]

    half = ech // 2
    lane = lax.broadcasted_iota(jnp.int32, (half, 128), 1)
    sub = lax.broadcasted_iota(jnp.int32, (half, 128), 0)
    lane16 = lax.broadcasted_iota(jnp.int32, (half // 2, 128), 1)
    lane1 = lax.broadcasted_iota(jnp.int32, (1, 128), 1)
    wlane = lax.broadcasted_iota(jnp.int32, (aug, 256), 1)

    @pl.loop(0, blocks, unroll=4)
    def _(b):
        start, count = meta_ref[0, b], meta_ref[1, b]
        slot, place, row = meta_ref[2, b], meta_ref[3, b], meta_ref[4, b]
        window = lax.shift_right_logical(start, 7)
        first = start & 127
        both = jnp.concatenate([emb[window], emb[window + 1]], axis=1)
        inside = (wlane >= first) & (wlane < first + count)
        masked = jnp.where(inside, both, jnp.zeros_like(both))
        padded = jnp.concatenate([both, jnp.zeros((128 - aug, 256), BF16)], axis=0)
        second = dot_nt(masked, padded)
        sums = second[ech:ech + 1, :]
        centred = second[0:ech, :] - second[0:ech, ech:ech + 1] * (sums * inv_ref[b])
        top, bottom = centred[0:half], centred[half:ech]
        folded = jnp.where((lane < half) & (lane < sub), pltpu.roll(bottom, 128 - half, 1), top)
        tile = jnp.where(lane16 < ech, folded[0:half // 2], pltpu.roll(folded[half // 2:], ech, 1))
        diag = jnp.sum(jnp.where(lane == sub + half, bottom, 0.0), axis=0, keepdims=True)
        extra = jnp.where(lane1 <= ech, sums, pltpu.roll(diag, ech, 1))
        extra = jnp.where(lane1 == ROW_LANE, row.astype(F32), extra)
        moments[pl.ds(place, 8, stride=slots), :] = tile[0:8]
        moments[pl.ds(place + 8 * slots, 8, stride=slots), :] = tile[8:16]
        extras[pl.ds(slot, 1), :] = extra

    @pl.loop(0, devices)
    def _(d):
        body = moments[pl.ds(pl.multiple_of(d * 16 * slots, 8), 16 * slots), :]
        out_ref[d, 0:16 * slots, :] = body.astype(BF16)
        extra = extras[pl.ds(pl.multiple_of(d * slots, 8), slots), :]
        high = extra.astype(BF16).astype(F32)
        both = jnp.concatenate([high, extra - high], axis=0)
        out_ref[d, 16 * slots:18 * slots, :] = both.astype(BF16)


def rows_kernel(dims, y_ref, mean_ref, cov_ref, extras, doubled, folded):
    devices, slots, sv, ech = dims
    half = ech // 2
    total = devices * slots
    row_of = lax.broadcasted_iota(jnp.int32, (2 * slots, 128), 0)
    col_of = lax.broadcasted_iota(jnp.int32, (2 * slots, 128), 1)
    step = jnp.where((row_of >= slots) & (col_of == ROW_LANE), float(sv), 0.0)

    @pl.loop(0, devices)
    def _(d):
        both = y_ref[d, 16 * slots:18 * slots, :].astype(F32)
        extra = both[0:slots] + both[slots:2 * slots]
        extras[pl.ds(pl.multiple_of(d * slots, 8), slots), :] = extra
        twice = jnp.concatenate([extra, extra], axis=0) + step
        doubled[pl.ds(pl.multiple_of(d * 2 * slots, 16), 2 * slots), :] = twice.astype(BF16)

    extra = extras[...]
    high = extra.astype(BF16)
    low = (extra - high.astype(F32)).astype(BF16)
    pick = jnp.where(lax.broadcasted_iota(jnp.int32, (8, 128), 1) == ROW_LANE, 1.0, 0.0).astype(BF16)
    row_line = dot_nt(pick, high)[0:1]
    hits = jnp.where(
        lax.broadcasted_iota(jnp.int32, (sv, total), 0).astype(F32) == row_line, 1.0, 0.0
    ).astype(BF16)
    totals = dot_nn(hits, high) + dot_nn(hits, low)
    count = totals[:, ech:ech + 1]
    inverse = 1.0 / jnp.maximum(count, 1.0)
    mean = totals * inverse
    mean_ref[...] = mean[:, 0:ech]

    lane_all = lax.broadcasted_iota(jnp.int32, (total, 128), 1)
    hits_t = jnp.where(lane_all.astype(F32) == extra[:, ROW_LANE:ROW_LANE + 1], 1.0, 0.0).astype(BF16)
    mean_a = mean.astype(BF16)
    rest = mean - mean_a.astype(F32)
    mean_b = rest.astype(BF16)
    mean_c = (rest - mean_b.astype(F32)).astype(BF16)
    own_mean = dot_nn(hits_t, mean_a) + dot_nn(hits_t, mean_b) + dot_nn(hits_t, mean_c)
    size = extra[:, ech:ech + 1]
    inv_size = jnp.where(size > 0.0, 1.0 / jnp.maximum(size, 1.0), 0.0)
    delta = jnp.where((lane_all < ech) & (size > 0.0), extra * inv_size - own_mean, 0.0)
    delta = delta + pltpu.roll(delta, ech, 1)
    weighted = (delta * size).astype(BF16)
    delta = delta.astype(BF16)
    eye = jnp.where(
        lax.broadcasted_iota(jnp.int32, (ech, 128), 0) == lax.broadcasted_iota(jnp.int32, (ech, 128), 1),
        1.0, 0.0,
    ).astype(BF16)
    lines = dot_nt(eye, weighted)

    pick_line = dot_nt(pick, doubled[...])[0:1]
    hits2 = jnp.where(
        lax.broadcasted_iota(jnp.int32, (2 * sv, 2 * total), 0).astype(F32) == pick_line, 1.0, 0.0
    ).astype(BF16)
    for p in range(half // 4):
        block = y_ref[:, p * 2 * slots:(p + 1) * 2 * slots, :].reshape(2 * total, 128)
        pair = dot_nn(hits2, block)
        for q in range(2):
            a = 2 * p + q
            turned = pair[q * sv:(q + 1) * sv].T
            folded[a * ech:(a + 1) * ech, :] = turned[0:ech]
            folded[(a + half // 2) * ech:(a + half // 2 + 1) * ech, :] = turned[ech:2 * ech]

    diag = totals.T[128 - half:128, :]
    sub8 = lax.broadcasted_iota(jnp.int32, (8, 128), 0)
    lane_sv = lax.broadcasted_iota(jnp.int32, (sv, 128), 1)

    def group(i, jg):
        j0 = jg * 8
        if i < half:
            ahead = folded[i * ech + j0:i * ech + j0 + 8, :]
            if j0 >= i:
                return ahead
            across = folded[pl.ds(j0 * ech + i, 8, stride=ech), :]
            if j0 + 7 < i:
                return across
            return jnp.where(sub8 + j0 >= i, ahead, across)
        if j0 < half:
            return folded[pl.ds(j0 * ech + i, 8, stride=ech), :]
        i2, j2 = i - half, j0 - half
        ahead = folded[i2 * ech + j2:i2 * ech + j2 + 8, :]
        if j2 + 7 < i2:
            return ahead
        across = folded[pl.ds(j2 * ech + i2, 8, stride=ech), :]
        if j2 > i2:
            return across
        mixed = jnp.where(sub8 + j2 < i2, ahead, across)
        return jnp.where(sub8 + j2 == i2, diag[i2:i2 + 1], mixed)

    for t in range(half):
        pieces = [group(2 * t + q, jg) for q in range(2) for jg in range(ech // 8)]
        within = jnp.concatenate(pieces, axis=0).T
        left = hits * lines[2 * t:2 * t + 1].astype(BF16)
        right = hits * lines[2 * t + 1:2 * t + 2].astype(BF16)
        between = jnp.where(lane_sv < ech, dot_nn(left, delta), dot_nn(right, delta))
        cov_ref[:, t * 128:(t + 1) * 128] = (within + between) * inverse


def permute(array, steps, sizes):
    axes = tuple(sizes)
    (na, nb) = (sizes[a] for a in axes)
    da, db = steps
    pairs = [
        (a * nb + b, (a + da) * nb + b + db)
        for a in range(na)
        for b in range(nb)
        if 0 <= a + da < na and 0 <= b + db < nb
    ]
    return lax.ppermute(array, axes, pairs)


def local(
    sizes, features, first_weight, first_bias, second_weight, second_bias, labels, blocks, owner_map
):
    channels, depth, rows, length = features.shape
    mid, ech = first_bias.shape[0], second_bias.shape[0]
    n_gz, n_xy = sizes["gz"], sizes["xy"]
    devices = n_gz * n_xy
    sv = owner_map.shape[0] // devices
    n_blocks, width = blocks.shape[2], blocks.shape[3]
    capacity = max(2, 3 * n_blocks // devices)
    slots = -(-capacity // 8) * 8

    grouped = regroup(features)
    edge = 2 * channels
    low_z, high_z = grouped[0:2], grouped[depth - 2:depth]
    low_y, high_y = grouped[:, 0:edge], grouped[:, rows * channels - edge:]
    below = permute(high_z, (1, 0), sizes)
    above = permute(low_z, (-1, 0), sizes)
    before = permute(high_y, (0, 1), sizes)
    after = permute(low_y, (0, -1), sizes)
    c00 = permute(high_y[depth - 2:], (1, 1), sizes)
    c01 = permute(low_y[depth - 2:], (1, -1), sizes)
    c10 = permute(high_y[0:2], (-1, 1), sizes)
    c11 = permute(low_y[0:2], (-1, -1), sizes)

    lists = blocks.reshape(n_blocks, width)
    starts = lists[:, 0]
    counts = jnp.sum((lists >= 0).astype(jnp.int32), axis=1)
    owner = owner_map[labels.reshape(-1)[starts]]
    target, row = owner // sv, owner % sv
    hits = (target[:, None] == jnp.arange(devices, dtype=jnp.int32)[None, :]).astype(jnp.int32)
    rank = jnp.sum((jnp.cumsum(hits, axis=0) - hits) * hits, axis=1)
    meta = jnp.stack([starts, counts, target * slots + rank, target * 16 * slots + rank, row])
    inv_counts = 1.0 / jnp.maximum(counts, 1).astype(F32)
    place = jnp.stack(
        [lax.axis_index("gz"), lax.axis_index("xy"), jnp.int32(n_gz - 1), jnp.int32(n_xy - 1)]
    ).astype(jnp.int32)

    w1 = first_weight.transpose(2, 3, 0, 1, 4).reshape(3 * mid, 9 * channels)
    w2 = second_weight.transpose(2, 3, 0, 1, 4).reshape(3 * ech, 9 * mid)
    b1 = jnp.broadcast_to(first_bias[:, None], (mid, length))
    b2 = jnp.broadcast_to(second_bias[:, None], (ech, length))

    smem = pl.BlockSpec(memory_space=pltpu.SMEM)
    vmem = pl.BlockSpec(memory_space=pltpu.VMEM)
    anywhere = pl.BlockSpec(memory_space=pl.ANY)
    dims = (depth, rows, channels, mid, ech, length, devices, slots, n_blocks)
    windows = depth * rows * length // 128
    packed = pl.pallas_call(
        functools.partial(tile_kernel, dims),
        out_shape=jax.ShapeDtypeStruct((devices, 18 * slots, 128), BF16),
        in_specs=[smem] * 3 + [anywhere] * 9 + [vmem] * 4,
        out_specs=vmem,
        scratch_shapes=[
            pltpu.VMEM((depth + 4, (rows + 4) * channels, length), BF16),
            pltpu.VMEM((depth + 2, (rows + 2) * mid, length), BF16),
            pltpu.VMEM((windows + 1, ech + 16, 128), BF16),
            pltpu.VMEM((devices * 16 * slots, 128), F32),
            pltpu.VMEM((devices * slots, 128), F32),
            pltpu.SemaphoreType.DMA((9,)),
        ],
        compiler_params=pltpu.CompilerParams(vmem_limit_bytes=56 << 20),
    )(meta, inv_counts, place, grouped, below, above, before, after, c00, c01, c10, c11, w1, w2, b1, b2)

    arrived = lax.all_to_all(packed, ("gz", "xy"), split_axis=0, concat_axis=0, tiled=True)

    total = devices * slots
    return pl.pallas_call(
        functools.partial(rows_kernel, (devices, slots, sv, ech)),
        out_shape=(
            jax.ShapeDtypeStruct((sv, ech), F32),
            jax.ShapeDtypeStruct((sv, ech * ech), F32),
        ),
        in_specs=[vmem],
        out_specs=(vmem, vmem),
        scratch_shapes=[
            pltpu.VMEM((total, 128), F32),
            pltpu.VMEM((2 * total, 128), BF16),
            pltpu.VMEM((ech // 2 * ech, 128), F32),
        ],
        compiler_params=pltpu.CompilerParams(vmem_limit_bytes=56 << 20),
    )(arrived)


def solution(mesh):
    sizes = {"gz": mesh.shape["gz"], "xy": mesh.shape["xy"]}
    return jax.shard_map(
        functools.partial(local, sizes),
        mesh=mesh,
        in_specs=(
            P(None, "gz", "xy", None),
            P(),
            P(),
            P(),
            P(),
            P("gz", "xy", None),
            P("gz", "xy", None, None),
            P(),
        ),
        out_specs=(P(("gz", "xy"), None), P(("gz", "xy"), None)),
        check_vma=False,
    )
```

time: 664 us -> 216 us (0.33); the launches traced: 656 us -> 216 us
  local copies, waits for them, and re-layouts: 342 us -> 15.5 us
  waiting for transfers between devices: 157 us -> 2.2 us
  blocking collectives: 0 us -> 89.7 us
  Pallas kernels: 0 us -> 81 us
  matrix products: 79.2 us -> 0 us
  starting transfers between devices: 50.2 us -> 24.5 us
  other arithmetic: 25.5 us -> 2.01 us
    gather x10 -> x2, local copies, waits for them, and re-layouts: 176 us -> 3.44 us  [local(): owner = owner_map[labels.reshape(-1)[starts]]]
    all_to_all x4 -> x0, waiting for transfers between devices: 143 us -> none  [the longest x1 143 us: local(): lax.all_to_all(send_second.reshape(devices, capacity, moment_width), ('gz...]
    conv_general_dilated x11 -> x0, local copies, waits for them, and re-layouts: 126 us -> none  [convolve(): lax.conv_general_dilated(padded[None], weight, (1, 1, 1), ((0, 0), (0, 0)...]
    all_to_all x0 -> x1, blocking collectives: none -> 89.7 us  [local(): lax.all_to_all(packed, ('gz', 'xy'), split_axis=0, concat_axis=0, tiled=T...]
    pallas_call x0 -> x3, Pallas kernels: none -> 81 us  [the longest x1 68.7 us: local(): pl.pallas_call(functools.partial(tile_kernel, dims), out_shape=jax.ShapeD...]
    conv_general_dilated x2 -> x0, matrix products: 60.7 us -> none  [convolve(): lax.conv_general_dilated(padded[None], weight, (1, 1, 1), ((0, 0), (0, 0)...]
    all_to_all x4 -> x0, starting transfers between devices: 28.3 us -> none  [the longest x1 9.4 us: local(): lax.all_to_all(send_sizes.reshape(devices, capacity), ('gz', 'xy'), split...]
    dot_general x4 -> x0, matrix products: 18.5 us -> none  [the longest x1 9.08 us: local(): jnp.einsum('cnk,dnk->ncd', picked, picked, preferred_element_type=jnp.flo...]
  transfers between devices with their start and end apart: 12 -> 8, of which waited for: 5 -> 1; matrix products, arithmetic and copies ran while one was open for 63% -> 5% of each run, Pallas kernels for 0% -> 0%
where the time goes in v1:
time: 216 us
  blocking collectives  89.7 us (42%)
  Pallas kernels  81 us (38%)
  starting transfers between devices  24.5 us (11%)
  local copies, waits for them, and re-layouts  15.5 us (7%)
  waiting for transfers between devices  2.2 us (1%)
    all_to_all x1, blocking collectives, local(): lax.all_to_all(packed, ('gz', 'xy'), split_axis=0, concat_axis=0, tiled=T...  89.7 us
    pallas_call x1, Pallas kernels, local(): pl.pallas_call(functools.partial(tile_kernel, dims), out_shape=jax.ShapeD...  68.7 us
    ppermute x8, starting transfers between devices, permute(): return lax.ppermute(array, axes, pairs)  24.5 us
    pallas_call x1, Pallas kernels, local(): pl.pallas_call(functools.partial(rows_kernel, (devices, slots, sv, ech)),...  9.95 us
  transfers between devices with their start and end apart: 8, of which 1 were waited for; matrix products, arithmetic and copies ran while one was open for 5% of the time, Pallas kernels for 0%

profile of v1, /device:TPU:0, one launch (start us, length us, event | category | flops | bytes accessed | tf_op | source)
XLA Modules:
  0.0 215.9 jit_solution(14321392433785850580)
XLA Ops:
  0.6 0.0 copy-start
  0.6 2.0 copy.17.x_ref
  2.7 2.3 %shard_map.95.centre = bf16[4,960,256]{2,1,0:T(8,128)(2,1)S(1)} custom-call(bf16[48,4,20,256]{3,2,1,0:T(8,128)(2,1)S(1)} %copy.17.x_ref), custom_call_target="tpu_custom_call" | custom-call | tf_op jit(solution)/shard_map/pallas_call | solution.py:37
  5.0 0.0 copy-start.1
  5.0 0.8 fusion.4
  5.8 1.3 collective-permute-start.7
  7.1 1.3 collective-permute-start.6
  8.4 1.4 collective-permute-start.5
  9.8 1.1 fusion.6
  10.9 1.3 collective-permute-start.1
  12.2 7.2 %collective-permute-start = (bf16[2,960,256]{2,1,0:T(8,128)(2,1)S(1)}, bf16[2,960,256]{2,1,0:T(8,128)(2,1)}, u32[]{:S(2)}, u32[]{:S(2)}) collective-permute-start(bf16[2,960,256]{2,1,0:T(8,128)(2,1)S(1)} %get-tuple-element.17), channel_id=1, source_target_pairs={{0,8},{1,9},{2,10},{3,11},{4,12},{5,13},{6,14},{7,15},{8,16},{9,17... | collective-permute-start | bytes 2949128 | tf_op jit(solution)/shard_map/ppermute | solution.py:281
  19.4 0.0 copy-done.8
  19.4 0.0 copy-done.5
  19.4 0.1 copy.14
  19.5 1.7 gather_fusion
  21.3 0.0 copy-start.2
  21.3 1.7 gather_fusion.1
  23.1 0.6 reduce-window.6
  23.7 0.2 slice_reduce_fusion
  23.9 0.1 fusion.2
  24.1 0.0 copy-done.1
  24.1 0.0 copy-start.9
  24.1 0.0 copy-start.10
  24.1 0.8 fusion.5
  24.9 0.0 collective-permute-done.7.c11
  24.9 1.3 collective-permute-start.3
  26.2 0.0 collective-permute-done.6.c10
  26.2 5.7 %collective-permute-start.2 = (bf16[4,96,256]{2,1,0:T(8,128)(2,1)}, bf16[4,96,256]{2,1,0:T(8,128)(2,1)S(1)}, u32[]{:S(2)}, u32[]{:S(2)}) collective-permute-start(bf16[4,96,256]{2,1,0:T(8,128)(2,1)} %get-tuple-element.15), channel_id=1, source_target_pairs={{0,1},{1,2},{2,3},{3,4},{4,5},{5,6},{6,7},{8,9},{9,10},{10,11},{11... | collective-permute-start | bytes 589832 | tf_op jit(solution)/shard_map/ppermute | solution.py:281
  32.0 0.6 convert_divide_fusion.inv_ref
  32.5 1.1 copy.18
  33.7 0.9 reshape.164.w1_ref
  34.6 0.3 copy.22
  34.9 1.0 reshape.182.w2_ref
  35.9 0.6 stack.19.meta_ref
  36.5 0.0 collective-permute-done.5.c01
  36.5 5.1 %collective-permute-start.4 = (bf16[2,96,256]{2,1,0:T(8,128)(2,1)S(1)}, bf16[2,96,256]{2,1,0:T(8,128)(2,1)S(1)}, u32[]{:S(2)}, u32[]{:S(2)}) collective-permute-start(bf16[2,96,256]{2,1,0:T(8,128)(2,1)S(1)} %copy-done.7), channel_id=1, source_target_pairs={{0,9},{1,10},{2,11},{3,12},{4,13},{5,14},{6,15},{8,17},{9,18},{10,... | collective-permute-start | bytes 294920 | tf_op jit(solution)/shard_map/ppermute | solution.py:281
  41.6 0.6 pad_add_fusion.place_ref
  42.2 2.2 %collective-permute-done.4.c00 = bf16[2,96,256]{2,1,0:T(8,128)(2,1)S(1)} collective-permute-done((bf16[2,96,256]{2,1,0:T(8,128)(2,1)S(1)}, bf16[2,96,256]{2,1,0:T(8,128)(2,1)S(1)}, u32[]{:S(2)}, u32[]{:S(2)}) %collective-permute-start.4) | collective-permute-done | bytes 98336 | tf_op jit(solution)/shard_map/ppermute | solution.py:281
  44.4 0.0 collective-permute-done.3.after
  44.4 0.0 collective-permute-done.2.before
  44.4 0.0 collective-permute-done.1.above
  44.5 0.0 collective-permute-done.below
  44.5 0.8 broadcast_in_dim.4.b1_ref
  45.3 0.7 broadcast_in_dim.5.b2_ref
  46.0 68.7 %shard_map.96 = bf16[32,432,128]{2,1,0:T(8,128)(2,1)} custom-call(s32[5,256]{1,0:T(8,128)} %stack.19.meta_ref, f32[256]{0:T(256)} %convert_divide_fusion.inv_ref, s32[4]{0:T(128)} %pad_add_fusion.place_ref, bf16[4,960,256]{2,1,0:T(8,128)(2,1)} %copy-done.1, bf16[2,960,256]{2,1,0:T(8,128)(2,1)} %collective-permute-done.below, ...), custom_call_target="tpu_custom_call" | custom-call | tf_op jit(solution)/shard_map/pallas_call | solution.py:332
  114.7 89.7 %all_to_all.5.y_ref = bf16[32,432,128]{2,1,0:T(8,128)(2,1)} all-to-all(bf16[32,432,128]{2,1,0:T(8,128)(2,1)} %shard_map.96), channel_id=1, replica_groups=mesh['gz'=4,'xy'=8] {'gz','xy'}, dimensions={0} | all-to-all | bytes 7077888 | tf_op jit(solution)/shard_map/all_to_all | solution.py:348
  204.4 9.9 %shard_map.97 = (f32[128,64]{1,0:T(8,128)}, f32[128,4096]{1,0:T(8,128)}) custom-call(bf16[32,432,128]{2,1,0:T(8,128)(2,1)} %all_to_all.5.y_ref), custom_call_target="tpu_custom_call" | custom-call | tf_op jit(solution)/shard_map/pallas_call | solution.py:351
  214.4 1.5 copy.21
  (29 shorter events, 0.2 us)
Async XLA Ops:
  0.6 20.7 %copy-start = (s32[4096]{0:T(1024)S(1)}, s32[4096]{0:T(1024)}, u32[]{:S(2)}) copy-start(s32[4096]{0:T(1024)} %param.15) | copy-start | bytes 49156
  5.0 19.1 %copy-start.1 = (bf16[4,960,256]{2,1,0:T(8,128)(2,1)}, bf16[4,960,256]{2,1,0:T(8,128)(2,1)S(1)}, u32[]{:S(2)}) copy-start(bf16[4,960,256]{2,1,0:T(8,128)(2,1)S(1)} %shard_map.95.centre) | copy-start | bytes 5898244
  5.8 19.1 %collective-permute-start.7 = (bf16[2,96,256]{2,1,0:T(8,128)(2,1)}, bf16[2,96,256]{2,1,0:T(8,128)(2,1)}, u32[]{:S(2)}, u32[]{:S(2)}) collective-permute-start(bf16[2,96,256]{2,1,0:T(8,128)(2,1)} %get-tuple-element.10), channel_id=1, source_target_pairs={{9,0},{10,1},{11,2},{12,3},{13,4},{14,5},{15,6},{17,8},{18,9},{19,... | collective-permute-start | bytes 294920 | tf_op jit(solution)/shard_map/ppermute | solution.py:281
  7.1 19.1 %collective-permute-start.6 = (bf16[2,96,256]{2,1,0:T(8,128)(2,1)}, bf16[2,96,256]{2,1,0:T(8,128)(2,1)}, u32[]{:S(2)}, u32[]{:S(2)}) collective-permute-start(bf16[2,96,256]{2,1,0:T(8,128)(2,1)} %get-tuple-element.11), channel_id=1, source_target_pairs={{8,1},{9,2},{10,3},{11,4},{12,5},{13,6},{14,7},{16,9},{17,10},{18,... | collective-permute-start | bytes 294920 | tf_op jit(solution)/shard_map/ppermute | solution.py:281
  8.4 11.0 %copy-start.8 = (s32[4,20,256]{2,0,1:T(4,128)S(1)}, s32[4,20,256]{2,0,1:T(4,128)}, u32[]{:S(2)}) copy-start(s32[4,20,256]{2,0,1:T(4,128)} %param.13) | copy-start | bytes 245764
  8.4 11.0 %copy-start.5 = (s32[1,1,256,128]{3,2,1,0:T(8,128)S(1)}, s32[1,1,256,128]{3,2,1,0:T(8,128)}, u32[]{:S(2)}) copy-start(s32[1,1,256,128]{3,2,1,0:T(8,128)} %param.14) | copy-start | bytes 393220
  8.4 28.1 %collective-permute-start.5 = (bf16[2,96,256]{2,1,0:T(8,128)(2,1)}, bf16[2,96,256]{2,1,0:T(8,128)(2,1)}, u32[]{:S(2)}, u32[]{:S(2)}) collective-permute-start(bf16[2,96,256]{2,1,0:T(8,128)(2,1)} %get-tuple-element.12), channel_id=1, source_target_pairs={{1,8},{2,9},{3,10},{4,11},{5,12},{6,13},{7,14},{9,16},{10,17},{11,... | collective-permute-start | bytes 294920 | tf_op jit(solution)/shard_map/ppermute | solution.py:281
  10.9 33.5 %collective-permute-start.1 = (bf16[2,960,256]{2,1,0:T(8,128)(2,1)}, bf16[2,960,256]{2,1,0:T(8,128)(2,1)}, u32[]{:S(2)}, u32[]{:S(2)}) collective-permute-start(bf16[2,960,256]{2,1,0:T(8,128)(2,1)} %get-tuple-element.16), channel_id=1, source_target_pairs={{8,0},{9,1},{10,2},{11,3},{12,4},{13,5},{14,6},{15,7},{16,8},{17,9... | collective-permute-start | bytes 2949128 | tf_op jit(solution)/shard_map/ppermute | solution.py:281
  12.2 32.3 %collective-permute-start = (bf16[2,960,256]{2,1,0:T(8,128)(2,1)S(1)}, bf16[2,960,256]{2,1,0:T(8,128)(2,1)}, u32[]{:S(2)}, u32[]{:S(2)}) collective-permute-start(bf16[2,960,256]{2,1,0:T(8,128)(2,1)S(1)} %get-tuple-element.17), channel_id=1, source_target_pairs={{0,8},{1,9},{2,10},{3,11},{4,12},{5,13},{6,14},{7,15},{8,16},{9,17... | collective-permute-start | bytes 2949128 | tf_op jit(solution)/shard_map/ppermute | solution.py:281
  21.3 13.3 %copy-start.2 = (bf16[3,3,3,64,48]{3,4,2,1,0:T(8,128)(2,1)S(1)}, bf16[3,3,3,64,48]{3,4,2,1,0:T(8,128)(2,1)}, u32[]{:S(2)}) copy-start(bf16[3,3,3,64,48]{3,4,2,1,0:T(8,128)(2,1)} %param.11) | copy-start | bytes 497668
  24.1 12.4 %copy-start.7 = (bf16[2,96,256]{2,1,0:T(8,128)(2,1)S(1)}, bf16[2,96,256]{2,1,0:T(8,128)(2,1)}, u32[]{:S(2)}) copy-start(bf16[2,96,256]{2,1,0:T(8,128)(2,1)} %get-tuple-element.13) | copy-start | bytes 294916
  24.1 20.4 %copy-start.9 = (f32[48]{0:T(128)S(1)}, f32[48]{0:T(128)}, u32[]{:S(2)}) copy-start(f32[48]{0:T(128)} %param.10) | copy-start | bytes 580
  24.1 21.2 %copy-start.10 = (f32[64]{0:T(128)S(1)}, f32[64]{0:T(128)}, u32[]{:S(2)}) copy-start(f32[64]{0:T(128)} %param.12) | copy-start | bytes 772
  24.9 19.5 %collective-permute-start.3 = (bf16[4,96,256]{2,1,0:T(8,128)(2,1)}, bf16[4,96,256]{2,1,0:T(8,128)(2,1)S(1)}, u32[]{:S(2)}, u32[]{:S(2)}) collective-permute-start(bf16[4,96,256]{2,1,0:T(8,128)(2,1)} %get-tuple-element.14), channel_id=1, source_target_pairs={{1,0},{2,1},{3,2},{4,3},{5,4},{6,5},{7,6},{9,8},{10,9},{11,10},{12... | collective-permute-start | bytes 589832 | tf_op jit(solution)/shard_map/ppermute | solution.py:281
  26.2 18.2 %collective-permute-start.2 = (bf16[4,96,256]{2,1,0:T(8,128)(2,1)}, bf16[4,96,256]{2,1,0:T(8,128)(2,1)S(1)}, u32[]{:S(2)}, u32[]{:S(2)}) collective-permute-start(bf16[4,96,256]{2,1,0:T(8,128)(2,1)} %get-tuple-element.15), channel_id=1, source_target_pairs={{0,1},{1,2},{2,3},{3,4},{4,5},{5,6},{6,7},{8,9},{9,10},{10,11},{11... | collective-permute-start | bytes 589832 | tf_op jit(solution)/shard_map/ppermute | solution.py:281
  36.5 7.9 %collective-permute-start.4 = (bf16[2,96,256]{2,1,0:T(8,128)(2,1)S(1)}, bf16[2,96,256]{2,1,0:T(8,128)(2,1)S(1)}, u32[]{:S(2)}, u32[]{:S(2)}) collective-permute-start(bf16[2,96,256]{2,1,0:T(8,128)(2,1)S(1)} %copy-done.7), channel_id=1, source_target_pairs={{0,9},{1,10},{2,11},{3,12},{4,13},{5,14},{6,15},{8,17},{9,18},{10,... | collective-permute-start | bytes 294920 | tf_op jit(solution)/shard_map/ppermute | solution.py:281
  44.4 1.5 copy-start.6
  44.4 1.5 copy-start.3
  44.4 1.5 copy-start.4
